TPU v7x, 128 devices: a whole 4x4x4 slice. The times are simulated.
128 devices in a mesh: dp: 32 (over z, y, x_hi), mod: 4 (over x_lo, core).
Axes of the slice: x: 4 (x_hi: 2, x_lo: 2; x = x_hi * 2 + x_lo), y: 4, z: 4, core: 2. Of those that a mesh axis runs over, the one named last changes fastest.
Arguments:
- embeddings: bfloat16 [4, 8192, 512], P('mod', 'dp'), may hold values from -4 to 4
- pairings: int32 [3, 4], replicated, may hold values from 0 to 3, as said below
- logit_scale: float32 [3], replicated, may hold values from 2 to 6
Outputs:
- gradient: float32 [4, 8192, 512], P('mod', 'dp')
- losses: float32 [4, 8192], P('mod', 'dp')
Inputs may be any that keep to these rules, and one draw needn't show every extreme that they name: Row k of pairings maps each modality to its partner in matching k; each row is an involution without fixed points, and the three rows are the three perfect matchings of the four modalities in some order.
All inputs are finite; a program needn't handle non-finite values.
Results may differ from a plain program's by a relative error of at most 0.0013.
Values may be sent and summed in bfloat16 or wider, within the bound.
A program may use at most 192 MiB of HBM per device.

v0:
```python
import jax
import jax.numpy as jnp
from jax import lax
from jax.sharding import PartitionSpec as P


def shards(embeddings, pairings, logit_scale):
    row_count = embeddings.shape[1]
    feat_width = embeddings.shape[2]
    mod_index = lax.axis_index("mod")
    anchor = embeddings[0]
    local_set = lax.all_gather(embeddings, "mod", axis=0, tiled=True)
    gradient = jnp.zeros((row_count, feat_width), jnp.float32)
    losses = jnp.zeros((row_count,), jnp.float32)
    for matching in range(3):
        partner_id = pairings[matching][mod_index]
        factor = logit_scale[matching]
        own_rows = lax.dynamic_index_in_dim(local_set, partner_id, 0, keepdims=False)
        partner = lax.all_gather(own_rows, "dp", axis=0, tiled=True)
        scores = factor * lax.dot_general(
            anchor, partner, (((1,), (1,)), ((), ())), preferred_element_type=jnp.float32
        )
        row_max = jnp.max(scores, 1, keepdims=True)
        row_lse = row_max[:, 0] + jnp.log(jnp.sum(jnp.exp(scores - row_max), 1))
        col_max = lax.pmax(jnp.max(scores, 0).astype(jnp.bfloat16), "dp").astype(jnp.float32)
        col_sum = lax.psum(jnp.sum(jnp.exp(scores - col_max[None, :]), 0), "dp")
        col_lse = col_max + jnp.log(col_sum)
        weights = (jnp.exp(scores - row_lse[:, None]) + jnp.exp(scores - col_lse[None, :])).astype(
            jnp.bfloat16
        )
        product = jnp.dot(weights, partner, preferred_element_type=jnp.float32)
        own_float = own_rows.astype(jnp.float32)
        diagonal = factor * jnp.sum(anchor.astype(jnp.float32) * own_float, -1)
        gradient = gradient + factor * (product - 2.0 * own_float)
        losses = losses + (row_lse - diagonal)
    return (gradient[None], losses[None])


def solution(mesh):
    return jax.shard_map(
        shards,
        mesh=mesh,
        in_specs=(P("mod", "dp", None), P(), P()),
        out_specs=(P("mod", "dp", None), P("mod", "dp")),
        check_vma=False,
    )
```

profile of v0, /device:TPU:0, one launch (start us, length us, event | category | flops | bytes accessed | tf_op | source)
XLA Modules:
  0.0 907.2 jit_solution(15729852674671141056)
XLA Ops:
  7.2 0.0 all-gather.8.cloned.1.call-start
  7.2 0.7 all-gather.8.cloned.1.call-update
  7.9 0.0 all-gather.14.cloned.1.call-start
  7.9 0.8 fusion.51
  8.7 0.7 constant_dynamic-slice_fusion.1
  12.1 0.6 constant_dynamic-slice_fusion.5
  16.0 16.9 %all-gather.8.cloned.1.call-done = bf16[4,256,512]{2,1,0:T(8,128)(2,1)} async-done(((bf16[1,256,512]{2,1,0:T(8,128)(2,1)}), bf16[4,256,512]{2,1,0:T(8,128)(2,1)}) %all-gather.8.cloned.1.call-update) | async-done | bytes 1048592 | tf_op jit(solution)/shard_map/all_gather | solution.py:12
  32.8 2.1 fusion.42
  34.9 0.0 all-gather.14.cloned.1.call-update
  35.0 0.0 all-gather.10.cloned.1.call-start
  35.0 0.7 all-gather.10.cloned.1.call-update
  35.7 0.0 all-gather.12.cloned.1.call-start
  35.7 0.5 all-gather.12.cloned.1.call-update
  36.3 0.0 all-reduce.4.cloned.1.call-start
  36.3 1.4 fusion.52
  37.7 103.0 %all-gather.14.cloned.1.call-done = bf16[1,8192,512]{2,1,0:T(8,128)(2,1)} async-done(((bf16[1,256,512]{2,1,0:T(8,128)(2,1)}), bf16[1,8192,512]{2,1,0:T(8,128)(2,1)}) %all-gather.14.cloned.1.call-update) | async-done | bytes 8388624 | tf_op jit(solution)/shard_map/all_gather | solution.py:19
  140.8 9.6 %fusion.50 = (f32[256]{0:T(256)S(1)}, bf16[8192]{0:T(1024)(128)(2,1)S(1)}, f32[8192,256]{1,0:T(8,128)}) fusion(bf16[1,256,512]{2,1,0:T(8,128)(2,1)} %param.3, bf16[1,8192,512]{2,1,0:T(8,128)(2,1)} %all-gather.14.cloned.1.call-done, f32[]{:T(128)} %bitcast.9), kind=kOutput, calls=%fused_computation.63 | convolution fusion | flops 2153766656 | bytes 17056772 | tf_op jit(solution)/shard_map/dot_general | solution.py:20
  150.4 95.9 %all-gather.10.cloned.1.call-done = bf16[1,8192,512]{2,1,0:T(8,128)(2,1)} async-done(((bf16[1,256,512]{2,1,0:T(8,128)(2,1)}), bf16[1,8192,512]{2,1,0:T(8,128)(2,1)}) %all-gather.10.cloned.1.call-update) | async-done | bytes 8388624 | tf_op jit(solution)/shard_map/all_gather | solution.py:19
  246.2 0.0 copy-done.1
  246.2 9.6 %fusion.48 = (f32[256]{0:T(256)S(1)}, bf16[8192]{0:T(1024)(128)(2,1)S(1)}, f32[8192,256]{1,0:T(8,128)}) fusion(bf16[1,256,512]{2,1,0:T(8,128)(2,1)S(1)} %copy-done.1, bf16[1,8192,512]{2,1,0:T(8,128)(2,1)} %all-gather.10.cloned.1.call-done, f32[]{:T(128)} %bitcast), kind=kOutput, calls=%fused_computation.61 | convolution fusion | flops 2153766656 | bytes 17056772 | tf_op jit(solution)/shard_map/dot_general | solution.py:20
  255.9 95.1 %all-gather.12.cloned.1.call-done = bf16[1,8192,512]{2,1,0:T(8,128)(2,1)} async-done(((bf16[1,256,512]{2,1,0:T(8,128)(2,1)}), bf16[1,8192,512]{2,1,0:T(8,128)(2,1)}) %all-gather.12.cloned.1.call-update) | async-done | bytes 8388624 | tf_op jit(solution)/shard_map/all_gather | solution.py:19
  351.0 9.6 %fusion.49 = (f32[256]{0:T(256)S(1)}, bf16[8192]{0:T(1024)(128)(2,1)S(1)}, f32[8192,256]{1,0:T(8,128)}) fusion(bf16[1,256,512]{2,1,0:T(8,128)(2,1)S(1)} %copy-done.1, bf16[1,8192,512]{2,1,0:T(8,128)(2,1)} %all-gather.12.cloned.1.call-done, f32[]{:T(128)} %bitcast.5), kind=kOutput, calls=%fused_computation.62 | convolution fusion | flops 2153766656 | bytes 17056772 | tf_op jit(solution)/shard_map/dot_general | solution.py:20
  360.6 180.2 %all-reduce.1 = (bf16[8192]{0:T(1024)(128)(2,1)S(1)}, bf16[8192]{0:T(1024)(128)(2,1)S(1)}, bf16[8192]{0:T(1024)(128)(2,1)S(1)}) all-reduce(bf16[8192]{0:T(1024)(128)(2,1)S(1)} %get-tuple-element.13, bf16[8192]{0:T(1024)(128)(2,1)S(1)} %get-tuple-element.9, ...), channel_id=1, replica_groups=mesh['dp'=32,'mod'=4] {'dp'}, use_global_device_ids=true, to_apply=%region_15.16 | all-reduce | flops 24576 | bytes 98304 | tf_op jit(solution)/shard_map/pmax | solution.py:25
  540.9 0.0 slice-start
  540.9 7.0 exponential_reduce_fusion.5
  547.8 0.0 copy-done
  547.8 4.2 exponential_reduce_fusion.3
  552.0 0.0 slice-done
  552.0 0.0 slice-done.1
  552.0 4.2 exponential_reduce_fusion.1
  556.2 0.0 all-reduce.4.cloned.1.call-update
  556.2 2.4 subtract_add_fusion
  558.6 312.2 %all-reduce.4.cloned.1.call-done = (f32[8192]{0:T(1024)}, f32[8192]{0:T(1024)}, f32[8192]{0:T(1024)}) async-done(((f32[8192]{0:T(1024)}, f32[8192]{0:T(1024)}, f32[8192]{0:T(1024)}), (f32[8192]{0:T(1024)}, f32[8192]{0:T(1024)}, f32[8192]{0:T(1024)})) %all-reduce.4.cloned.1.call-update) | async-done | bytes 98320 | tf_op jit(solution)/shard_map/psum | solution.py:26
  870.8 0.8 log_add_fusion.2
  871.6 0.8 log_add_fusion.1
  872.4 0.8 log_add_fusion
  873.2 0.0 copy-done.4
  873.2 0.0 copy-start.3
  873.2 0.0 slice-start.2
  873.2 0.0 slice-start.4
  873.2 10.3 %fusion.33 = f32[256,512]{1,0:T(8,128)S(1)} fusion(bf16[1,8192,512]{2,1,0:T(8,128)(2,1)} %all-gather.12.cloned.1.call-done, f32[8192,256]{1,0:T(8,128)} %get-tuple-element.37, f32[8192]{0:T(1024)S(1)} %log_add_fusion.1, f32[256]{0:T(256)S(1)} %get-tuple-element.25, bf16[1,256,512]{2,1,0:T(8,128)(2,1)S(1)} %copy-done.4, f32[]{:T(128)} %bitcast.5), kind=kOutput, calls=%fused_computation.33 | convolution fusion | flops 2156396544 | bytes 17597444 | tf_op jit(solution)/shard_map/dot_general | solution.py:31
  883.5 0.0 slice-start.3
  883.5 0.0 slice-start.5
  883.5 0.0 copy-done.3
  883.5 0.0 copy-start.2
  883.5 10.4 %fusion.39 = f32[256,512]{1,0:T(8,128)S(1)} fusion(bf16[1,8192,512]{2,1,0:T(8,128)(2,1)} %all-gather.14.cloned.1.call-done, f32[8192,256]{1,0:T(8,128)} %get-tuple-element.36, f32[8192]{0:T(1024)S(1)} %log_add_fusion, f32[256]{0:T(256)S(1)} %get-tuple-element.26, bf16[1,256,512]{2,1,0:T(8,128)(2,1)S(1)} %copy-done.3, f32[]{:T(128)} %bitcast.9), kind=kOutput, calls=%fused_computation.35 | convolution fusion | flops 2156396544 | bytes 17597444 | tf_op jit(solution)/shard_map/dot_general | solution.py:31
  893.9 0.0 slice-done.2
  894.0 6.7 fusion.27
  (14 shorter events, 0.0 us)
Async XLA Ops:
  7.2 25.7 %all-gather.8.cloned.1.call-start = ((), (), s32[]{:S(2)}) async-start(), calls=%async_computation | async-start | bytes 1310720 | tf_op jit(solution)/shard_map/all_gather | solution.py:12
  7.9 132.9 %all-gather.14.cloned.1.call-start = ((), (), s32[]{:S(2)}) async-start(), calls=%async_computation.3 | async-start | bytes 8650752 | tf_op jit(solution)/shard_map/all_gather | solution.py:19
  35.0 211.3 %all-gather.10.cloned.1.call-start = ((), (), s32[]{:S(2)}) async-start(), calls=%async_computation.1 | async-start | bytes 8650752 | tf_op jit(solution)/shard_map/all_gather | solution.py:19
  35.7 315.3 %all-gather.12.cloned.1.call-start = ((), (), s32[]{:S(2)}) async-start(), calls=%async_computation.2 | async-start | bytes 8650752 | tf_op jit(solution)/shard_map/all_gather | solution.py:19
  36.3 834.6 %all-reduce.4.cloned.1.call-start = ((), (), s32[]{:S(2)}) async-start(), calls=%async_computation.4 | async-start | bytes 196608 | tf_op jit(solution)/shard_map/psum | solution.py:26
  140.7 105.5 %copy-start.1 = (bf16[1,256,512]{2,1,0:T(8,128)(2,1)S(1)}, bf16[1,256,512]{2,1,0:T(8,128)(2,1)}, u32[]{:S(2)}) copy-start(bf16[1,256,512]{2,1,0:T(8,128)(2,1)} %param.3) | copy-start | bytes 786436
  540.8 7.0 copy-start
  540.9 11.2 %slice-start = ((s8[8388608]{0:T(1024)(128)(4,1)}), s8[4194304]{0:T(1024)(128)(4,1)S(1)}, s32[]{:S(2)}) async-start(s8[8388608]{0:T(1024)(128)(4,1)} %bitcast.76), calls=%async_computation.5 | async-start | bytes 8388608
  547.8 4.2 slice-start.1
  547.8 325.3 %copy-start.4 = (bf16[1,256,512]{2,1,0:T(8,128)(2,1)S(1)}, bf16[1,256,512]{2,1,0:T(8,128)(2,1)}, u32[]{:S(2)}) copy-start(bf16[1,256,512]{2,1,0:T(8,128)(2,1)} %get-tuple-element.28) | copy-start | bytes 786436
  873.2 10.3 %copy-start.3 = (bf16[1,256,512]{2,1,0:T(8,128)(2,1)S(1)}, bf16[1,256,512]{2,1,0:T(8,128)(2,1)}, u32[]{:S(2)}) copy-start(bf16[1,256,512]{2,1,0:T(8,128)(2,1)} %get-tuple-element.29) | copy-start | bytes 786436
  873.2 20.7 %slice-start.2 = ((s8[8388608]{0:T(1024)(128)(4,1)}), s8[4194304]{0:T(1024)(128)(4,1)S(1)}, s32[]{:S(2)}) async-start(s8[8388608]{0:T(1024)(128)(4,1)} %bitcast.78), calls=%async_computation.7 | async-start | bytes 8388608
  873.2 20.7 %slice-start.4 = ((s8[8388608]{0:T(1024)(128)(4,1)}), s8[4194304]{0:T(1024)(128)(4,1)S(1)}, s32[]{:S(2)}) async-start(s8[8388608]{0:T(1024)(128)(4,1)} %bitcast.81), calls=%async_computation.9 | async-start | bytes 8388608
  883.5 10.5 %slice-start.3 = ((s8[8388608]{0:T(1024)(128)(4,1)}), s8[4194304]{0:T(1024)(128)(4,1)S(1)}, s32[]{:S(2)}) async-start(s8[8388608]{0:T(1024)(128)(4,1)} %bitcast.78), calls=%async_computation.8 | async-start | bytes 8388608
  883.5 10.5 %slice-start.5 = ((s8[8388608]{0:T(1024)(128)(4,1)}), s8[4194304]{0:T(1024)(128)(4,1)S(1)}, s32[]{:S(2)}) async-start(s8[8388608]{0:T(1024)(128)(4,1)} %bitcast.81), calls=%async_computation.10 | async-start | bytes 8388608
  883.5 10.4 %copy-start.2 = (bf16[1,256,512]{2,1,0:T(8,128)(2,1)S(1)}, bf16[1,256,512]{2,1,0:T(8,128)(2,1)}, u32[]{:S(2)}) copy-start(bf16[1,256,512]{2,1,0:T(8,128)(2,1)} %get-tuple-element.27) | copy-start | bytes 786436
Sparse Core Ops, SparseCore 0:
  9.7 23.1 all-gather.7
  35.9 104.8 all-gather.13
  144.4 101.7 all-gather.9
  249.2 101.7 all-gather.11
  556.3 314.4 all-reduce.3
where the time goes:
time: 908 us; the launch traced here: 907 us
  waiting for transfers between devices  625 us (69%)
  blocking collectives  180 us (20%)
  matrix products  56.1 us (6%)
  other arithmetic  22.1 us (2%)
  between operations  19.9 us (2%)
    psum x1, waiting for transfers between devices, shards(): col_sum = lax.psum(jnp.sum(jnp.exp(scores - col_max[None, :]), 0), 'dp')  312 us
    all_gather x3, waiting for transfers between devices, shards(): partner = lax.all_gather(own_rows, 'dp', axis=0, tiled=True)  294 us
    pmax x1, blocking collectives, shards(): lax.pmax(jnp.max(scores, 0).astype(jnp.bfloat16), 'dp').astype(jnp.float32)  180 us
    dot_general x3, matrix products, shards(): lax.dot_general(anchor, partner, (((1,), (1,)), ((), ())), preferred_elem...  28.8 us
    dot_general x3, matrix products, shards(): product = jnp.dot(weights, partner, preferred_element_type=jnp.float32)  27.3 us
  transfers between devices with their start and end apart: 5, of which 5 were waited for; matrix products, arithmetic and copies ran while one was open for 3% of the time, Pallas kernels for 0%

commit v1 on v0

v1 whole, which is shorter than its diff:
```python
import jax
import jax.numpy as jnp
from jax import lax
from jax.sharding import PartitionSpec as P


def shards(embeddings, pairings, logit_scale):
    row_count = embeddings.shape[1]
    feat_width = embeddings.shape[2]
    mod_index = lax.axis_index("mod")
    anchor = embeddings[0]
    local_set = lax.all_gather(embeddings, "mod", axis=0, tiled=True)
    everything = lax.all_gather(local_set, "dp", axis=1, tiled=True)
    scores = []
    row_lse = []
    partners = []
    for matching in range(3):
        partner_id = pairings[matching][mod_index]
        partner = lax.dynamic_index_in_dim(everything, partner_id, 0, keepdims=False)
        score = logit_scale[matching] * lax.dot_general(
            anchor, partner, (((1,), (1,)), ((), ())), preferred_element_type=jnp.float32
        )
        row_max = jnp.max(score, 1, keepdims=True)
        row_lse.append(row_max[:, 0] + jnp.log(jnp.sum(jnp.exp(score - row_max), 1)))
        scores.append(score)
        partners.append(partner)
    stats = lax.all_gather(lax.all_gather(jnp.stack(row_lse)[None], "mod", axis=0, tiled=True), "dp", axis=2, tiled=True)
    gradient = jnp.zeros((row_count, feat_width), jnp.float32)
    losses = jnp.zeros((row_count,), jnp.float32)
    for matching in range(3):
        partner_id = pairings[matching][mod_index]
        factor = logit_scale[matching]
        own_rows = lax.dynamic_index_in_dim(local_set, partner_id, 0, keepdims=False)
        col_lse = lax.dynamic_index_in_dim(stats, partner_id, 0, keepdims=False)[matching]
        score = scores[matching]
        weights = (jnp.exp(score - row_lse[matching][:, None]) + jnp.exp(score - col_lse[None, :])).astype(jnp.bfloat16)
        product = jnp.dot(weights, partners[matching], preferred_element_type=jnp.float32)
        own_float = own_rows.astype(jnp.float32)
        diagonal = factor * jnp.sum(anchor.astype(jnp.float32) * own_float, -1)
        gradient = gradient + factor * (product - 2.0 * own_float)
        losses = losses + (row_lse[matching] - diagonal)
    return (gradient[None], losses[None])


def solution(mesh):
    return jax.shard_map(
        shards,
        mesh=mesh,
        in_specs=(P("mod", "dp", None), P(), P()),
        out_specs=(P("mod", "dp", None), P("mod", "dp")),
        check_vma=False,
    )
```

time: 908 us -> 457 us (0.50)
  waiting for transfers between devices: 625 us -> 279 us
  blocking collectives: 180 us -> 100 us
  other arithmetic: 22.1 us -> 7.41 us
  matrix products: 56.1 us -> 45.8 us
    psum x1 -> x0, waiting for transfers between devices: 312 us -> none  [shards(): col_sum = lax.psum(jnp.sum(jnp.exp(scores - col_max[None, :]), 0), 'dp')]
    pmax x1 -> x0, blocking collectives: 180 us -> none  [shards(): lax.pmax(jnp.max(scores, 0).astype(jnp.bfloat16), 'dp').astype(jnp.float32)]
    all_gather x0 -> x2, blocking collectives: none -> 100 us  [the longest x1 95 us: shards(): lax.all_gather(lax.all_gather(jnp.stack(row_lse)[None], 'mod', axis=0, ti...]
    all_gather x3 -> x1, waiting for transfers between devices: 294 us -> 254 us  [shards(): everything = lax.all_gather(local_set, 'dp', axis=1, tiled=True)]
    reduce_sum x3, other arithmetic: 15.3 us -> 3.5 us  [shards(): jnp.sum(jnp.exp(score - row_max), 1)]
    dot_general x3, matrix products: 28.8 us -> 19.2 us  [shards(): lax.dot_general(anchor, partner, (((1,), (1,)), ((), ())), preferred_elem...]
  transfers between devices with their start and end apart: 5 -> 2, of which waited for: 5 -> 2; matrix products, arithmetic and copies ran while one was open for 3% -> 1% of each run, Pallas kernels for 0% -> 0%
where the time goes in v1:
time: 457 us; the launch traced here: 456 us
  waiting for transfers between devices  279 us (61%)
  blocking collectives  100 us (22%)
  matrix products  45.8 us (10%)
  between operations  19.9 us (4%)
  other arithmetic  7.41 us (2%)
    all_gather x1, waiting for transfers between devices, shards(): everything = lax.all_gather(local_set, 'dp', axis=1, tiled=True)  254 us
    all_gather x1, blocking collectives, shards(): lax.all_gather(lax.all_gather(jnp.stack(row_lse)[None], 'mod', axis=0, ti...  95 us
    dot_general x3, matrix products, shards(): jnp.dot(weights, partners[matching], preferred_element_type=jnp.float32)  26.6 us
    all_gather x1, waiting for transfers between devices, shards(): local_set = lax.all_gather(embeddings, 'mod', axis=0, tiled=True)  24.9 us
    dot_general x3, matrix products, shards(): lax.dot_general(anchor, partner, (((1,), (1,)), ((), ())), preferred_elem...  19.2 us
  transfers between devices with their start and end apart: 2, of which 2 were waited for; matrix products, arithmetic and copies ran while one was open for 1% of the time, Pallas kernels for 0%

profile of v1, /device:TPU:0, one launch (start us, length us, event | category | flops | bytes accessed | tf_op | source)
XLA Modules:
  0.0 455.9 jit_solution(3657351829678771458)
XLA Ops:
  7.2 0.0 all-gather.5.cloned.1.call-start
  7.2 0.7 all-gather.5.cloned.1.call-update
  7.9 0.0 all-gather.7.cloned.1.call-start
  7.9 24.9 %all-gather.5.cloned.1.call-done = bf16[4,256,512]{2,1,0:T(8,128)(2,1)} async-done(((bf16[1,256,512]{2,1,0:T(8,128)(2,1)}), bf16[4,256,512]{2,1,0:T(8,128)(2,1)}) %all-gather.5.cloned.1.call-update) | async-done | bytes 1048592 | tf_op jit(solution)/shard_map/all_gather | solution.py:12
  32.8 0.0 all-gather.7.cloned.1.call-update
  32.8 0.8 fusion.60
  33.6 0.6 constant_dynamic-slice_fusion.3
  36.8 0.6 constant_dynamic-slice_fusion.5
  40.6 1.4 fusion.61
  42.0 1.4 fusion.48
  43.4 0.7 broadcast_multiply_fusion
  44.1 0.6 broadcast_multiply_fusion.1
  44.7 0.6 broadcast_multiply_fusion.2
  45.3 253.5 %all-gather.7.cloned.1.call-done = bf16[4,8192,512]{2,1,0:T(8,128)(2,1)} async-done(((bf16[4,256,512]{2,1,0:T(8,128)(2,1)}), bf16[4,8192,512]{2,1,0:T(8,128)(2,1)}) %all-gather.7.cloned.1.call-update) | async-done | bytes 33554448 | tf_op jit(solution)/shard_map/all_gather | solution.py:13
  298.9 6.4 %fusion.62 = (f32[256]{0:T(256)S(1)}, f32[8192,256]{1,0:T(8,128)S(1)}) fusion(bf16[1,256,512]{2,1,0:T(8,128)(2,1)} %param.3, bf16[4,8192,512]{2,1,0:T(8,128)(2,1)} %all-gather.7.cloned.1.call-done, s32[]{:T(128)S(6)} %select_n.29, f32[]{:T(128)} %bitcast.9), kind=kOutput, calls=%fused_computation.73 | convolution fusion | flops 2151677696 | bytes 17040900 | tf_op jit(solution)/shard_map/dot_general | solution.py:20
  305.3 0.0 copy-start
  305.3 1.2 exponential_reduce_fusion
  306.5 0.0 copy-done
  306.5 6.4 %fusion.63 = (f32[256]{0:T(256)S(1)}, f32[8192,256]{1,0:T(8,128)S(1)}) fusion(bf16[1,256,512]{2,1,0:T(8,128)(2,1)S(1)} %copy-done, bf16[4,8192,512]{2,1,0:T(8,128)(2,1)} %all-gather.7.cloned.1.call-done, s32[]{:T(128)S(6)} %select_n.28, f32[]{:T(128)} %bitcast.5), kind=kOutput, calls=%fused_computation.74 | convolution fusion | flops 2151677696 | bytes 17040900 | tf_op jit(solution)/shard_map/dot_general | solution.py:20
  312.8 1.2 exponential_reduce_fusion.1
  314.0 6.4 %fusion.64 = (f32[256]{0:T(256)S(1)}, f32[8192,256]{1,0:T(8,128)S(1)}) fusion(bf16[1,256,512]{2,1,0:T(8,128)(2,1)S(1)} %copy-done, bf16[4,8192,512]{2,1,0:T(8,128)(2,1)} %all-gather.7.cloned.1.call-done, s32[]{:T(128)S(6)} %select_n.27, f32[]{:T(128)} %bitcast), kind=kOutput, calls=%fused_computation.75 | convolution fusion | flops 2151677696 | bytes 17040900 | tf_op jit(solution)/shard_map/dot_general | solution.py:20
  320.4 0.0 copy-start.1
  320.4 1.2 exponential_reduce_fusion.2
  321.6 5.2 %all-gather.1 = f32[4,3,256]{2,1,0:T(4,128)S(1)} all-gather(f32[1,3,256]{2,1,0:T(4,128)S(1)} %maximum_bitcast_fusion), channel_id=2, replica_groups=mesh['dp'=32,'mod'=4] {'mod'}, dimensions={0}, use_global_device_ids=true | all-gather | bytes 15360 | tf_op jit(solution)/shard_map/all_gather | solution.py:27
  326.8 95.0 %all_gather.15 = f32[4,3,8192]{2,1,0:T(4,128)S(1)} all-gather(f32[4,3,256]{2,1,0:T(4,128)S(1)} %all-gather.1), channel_id=1, replica_groups=mesh['dp'=32,'mod'=4] {'dp'}, dimensions={2}, use_global_device_ids=true | all-gather | bytes 405504 | tf_op jit(solution)/shard_map/all_gather | solution.py:27
  421.8 0.1 constant_dynamic-slice_fusion.2
  421.9 0.6 subtract_add_fusion
  422.4 0.0 copy-done.1
  422.4 8.6 %fusion.45 = f32[256,512]{1,0:T(8,128)S(1)} fusion(bf16[4,8192,512]{2,1,0:T(8,128)(2,1)} %all-gather.7.cloned.1.call-done, s32[]{:T(128)S(6)} %select_n.29, f32[8192,256]{1,0:T(8,128)S(1)} %get-tuple-element.15, f32[8192]{0:T(1024)S(1)} %bitcast.88, f32[256]{0:T(256)S(1)} %log_add_fusion, f32[]{:T(128)} %bitcast.9, bf16[4,256,512]{2,1,0:T(8,128)(2,1)S(1)} %copy-done.1), kind=kOutput, calls=%fused_computation.38 | convolution fusion | flops 2156396544 | bytes 17598976 | tf_op jit(solution)/shard_map/dot_general | solution.py:37
  431.1 8.6 %fusion.39 = f32[256,512]{1,0:T(8,128)S(1)} fusion(bf16[4,8192,512]{2,1,0:T(8,128)(2,1)} %all-gather.7.cloned.1.call-done, s32[]{:T(128)S(6)} %select_n.28, f32[8192,256]{1,0:T(8,128)S(1)} %get-tuple-element.17, f32[8192]{0:T(1024)S(1)} %bitcast.87, f32[256]{0:T(256)S(1)} %log_add_fusion.1, f32[]{:T(128)} %bitcast.5, bf16[4,256,512]{2,1,0:T(8,128)(2,1)S(1)} %copy-done.1), kind=kOutput, calls=%fused_computation.36 | convolution fusion | flops 2156396544 | bytes 17598976 | tf_op jit(solution)/shard_map/dot_general | solution.py:37
  439.6 9.5 %fusion.33 = f32[1,256,512]{2,1,0:T(8,128)} fusion(f32[256,512]{1,0:T(8,128)S(1)} %fusion.45, f32[256,512]{1,0:T(8,128)S(1)} %fusion.39, bf16[4,8192,512]{2,1,0:T(8,128)(2,1)} %all-gather.7.cloned.1.call-done, s32[]{:T(128)S(6)} %select_n.27, f32[8192,256]{1,0:T(8,128)S(1)} %get-tuple-element.19, f32[8192]{0:T(1024)S(1)} %bitcast.86, ...), kind=kOutput, calls=%fused_computation.34 | convolution fusion | flops 2156658688 | bytes 18647552 | tf_op jit(solution)/shard_map/dot_general | solution.py:37
  (4 shorter events, 0.0 us)
Async XLA Ops:
  7.2 25.7 %all-gather.5.cloned.1.call-start = ((), (), s32[]{:S(2)}) async-start(), calls=%async_computation | async-start | bytes 1310720 | tf_op jit(solution)/shard_map/all_gather | solution.py:12
  7.9 291.0 %all-gather.7.cloned.1.call-start = ((), (), s32[]{:S(2)}) async-start(), calls=%async_computation.1 | async-start | bytes 34603008 | tf_op jit(solution)/shard_map/all_gather | solution.py:13
  305.3 1.2 copy-start
  320.4 102.0 %copy-start.1 = (bf16[4,256,512]{2,1,0:T(8,128)(2,1)S(1)}, bf16[4,256,512]{2,1,0:T(8,128)(2,1)}, u32[]{:S(2)}) copy-start(bf16[4,256,512]{2,1,0:T(8,128)(2,1)} %all-gather.5.cloned.1.call-done) | copy-start | bytes 3145732
Sparse Core Ops, SparseCore 0:
  9.7 23.1 all-gather.4
  35.9 262.8 all-gather.6

commit v2 on v0

v2 whole, which is shorter than its diff:
```python
import functools
import math

import jax
import jax.numpy as jnp
from jax import lax
from jax.experimental import pallas as pl
from jax.experimental.pallas import tpu as pltpu
from jax.sharding import PartitionSpec as P

MESH = pl.DeviceIdType.MESH
F32 = jnp.float32
BF16 = jnp.bfloat16
LN2 = math.log(2.0)
LOG2E = 1.0 / LN2
PART = F32


def kernel(
    pair_ref, scale_ref, emb_ref, grad_ref, loss_ref,
    cols, rows, scores, run_max, run_sum, acc, stage, relay, final,
    part, own_lse, col_lse, row_lse,
    local_sem, ag_send, ag_recv, sib_send, sib_recv, row_send, row_recv,
    part_send, part_recv, lse_send, lse_recv, rs_send, rs_recv,
):
    count, width = emb_ref.shape
    half, quarter = count // 2, count // 4
    dp = lax.axis_index("dp")
    mod = lax.axis_index("mod")
    x_hi, y, z = dp % 2, (dp // 2) % 4, dp // 8
    core, x_lo = mod % 2, mod // 2
    x = x_hi * 2 + x_lo

    def device(dx=0, dy=0, dz=0, dc=0):
        xx, yy, zz, cc = (x + dx) % 4, (y + dy) % 4, (z + dz) % 4, (core + dc) % 2
        return {"dp": (zz * 4 + yy) * 2 + xx // 2, "mod": (xx % 2) * 2 + cc}

    def partner(q):
        return ((x_lo + q // 2) % 2) * 2 + (core + q % 2) % 2

    def factor(q):
        p = partner(q)
        total = jnp.float32(0.0)
        for k in range(3):
            total = total + jnp.where(pair_ref[k, mod] == p, scale_ref[k], jnp.float32(0.0))
        return total

    def remote(src, dst, send, recv, to):
        return pltpu.make_async_remote_copy(
            src_ref=src, dst_ref=dst, send_sem=send, recv_sem=recv, device_id=to, device_id_type=MESH
        )

    barrier = pltpu.get_barrier_semaphore()
    peers = [device(dz=1), device(dz=3), device(dy=1), device(dy=2), device(dy=3)]
    for q in (1, 2, 3):
        for block in range(8):
            peers.append({"dp": ((block % 4) * 4 + y) * 2 + block // 4, "mod": partner(q)})
    for peer in peers:
        pl.semaphore_signal(barrier, inc=1, device_id=peer, device_id_type=MESH)

    def block_of(dx, dz):
        xx, zz = (x + dx) % 4, (z + dz) % 4
        return xx % 2, (xx // 2) * 4 + zz

    def piece(dx, dz, start, size, dc=0):
        lo, block = block_of(dx, dz)
        return cols.at[lo * 2 + (core + dc) % 2, pl.ds(pl.multiple_of(block * count + start, 64), size), :]

    fill_cols = pltpu.make_async_copy(emb_ref, piece(0, 0, 0, count), local_sem.at[0])
    fill_rows = pltpu.make_async_copy(emb_ref, rows.at[y], local_sem.at[1])
    fill_cols.start()
    fill_rows.start()
    run_max[...] = jnp.full(run_max.shape, -1e30, F32)
    run_sum[...] = jnp.zeros(run_sum.shape, F32)
    pl.semaphore_wait(barrier, len(peers))

    EVENTS = ((-1, 0, half, 1), (1, 0, half, -1), (2, 0, quarter, 1), (2, quarter, quarter, -1))

    def offsets(h, a, b):
        return (a, b) if h == 0 else (b, a)

    def place(h, group, event):
        rel, start, size, way = EVENTS[event]
        a, b = (rel, 0) if group == 0 else ((0, -1, 1, 2)[group - 1], rel)
        dx, dz = offsets(h, a, b)
        along_x = (group == 0) == (h == 0)
        return dx, dz, h * half + start, size, way, along_x

    def ag_copy(h, group, event):
        dx, dz, start, size, way, along_x = place(h, group, event)
        to = device(dx=way) if along_x else device(dz=way)
        sx, sz = (dx + way, dz) if along_x else (dx, dz + way)
        src = piece(sx, sz, start, size)
        if group in (0, 1) and event in (0, 1):
            src = emb_ref.at[pl.ds(start, size), :]
        return remote(src, piece(sx, sz, start, size), ag_send.at[h, group, event], ag_recv.at[h, group, event], to)

    def ag_arrival(h, group, event):
        dx, dz, start, size, _, _ = place(h, group, event)
        region = piece(dx, dz, start, size)
        return remote(region, region, ag_send.at[h, group, event], ag_recv.at[h, group, event], device(dc=1))

    def sib_copy(h, group, event, dc=0):
        dx, dz, start, size, _, _ = place(h, group, event)
        region = piece(dx, dz, start, size, dc)
        return remote(region, region, sib_send.at[h, group, event], sib_recv.at[h, group, event], device(dc=1))

    def sib_own(dc=0):
        region = piece(0, 0, 0, count, dc)
        src = region if dc else emb_ref
        return remote(src, region, sib_send.at[0, 5, 0], sib_recv.at[0, 5, 0], device(dc=1))

    row_spans = ((1, 0, count, 1), (-1, 0, count, -1), (2, 0, half, 1), (2, half, half, -1))

    def row_copy(event, arrival=False):
        rel, start, size, way = row_spans[event]
        owner = y - way if event >= 2 else y
        if arrival:
            owner = y + (2 if event >= 2 else -way)
        region = rows.at[(owner + 4) % 4, pl.ds(start, size), :]
        src = emb_ref if event < 2 and not arrival else region
        return remote(src, region, row_send.at[event], row_recv.at[event], device(dy=way))

    started = []

    def go(copy):
        copy.start()
        started.append(copy)

    def forward_to_sibling(group, events):
        for h in (0, 1):
            for event in events:
                go(sib_copy(h, group, event))

    def arrive(group, events):
        for h in (0, 1):
            for event in events:
                ag_arrival(h, group, event).wait_recv()

    def send(group, events):
        for h in (0, 1):
            for event in events:
                go(ag_copy(h, group, event))

    def sib_arrive(group, events):
        for h in (0, 1):
            for event in events:
                sib_copy(h, group, event, 1).wait_recv()

    def units(n, decode):
        def body(step, carry):
            i, r = step // 4, step % 4
            q, dx, dz = decode(i)
            lo, block = block_of(dx, dz)
            p = partner(q)
            scale = factor(q) * jnp.float32(LOG2E)
            here = pl.ds(pl.multiple_of(block * count, count), count)
            these = pl.ds(pl.multiple_of(r * count, count), count)
            t = scale * lax.dot_general(
                rows[r], cols[p, here, :], (((1,), (1,)), ((), ())), preferred_element_type=F32
            )
            scores[q - 1, these, here] = t
            old = run_max[q - 1, these, :]
            new = old
            for lane in range(0, count, 128):
                new = jnp.maximum(new, t[:, lane:lane + 128])
            total = run_sum[q - 1, these, :] * jnp.exp2(old - new)
            for lane in range(0, count, 128):
                total = total + jnp.exp2(t[:, lane:lane + 128] - new)
            run_max[q - 1, these, :] = new
            run_sum[q - 1, these, :] = total
            return carry

        lax.fori_loop(0, n * 4, body, 0)

    near, far = (0, 1), (2, 3)
    send(0, near)
    go(sib_own())
    go(row_copy(0))
    go(row_copy(1))
    send(1, near)
    fill_cols.wait()
    fill_rows.wait()
    arrive(0, near)
    send(0, far)
    send(2, near)
    send(3, near)
    forward_to_sibling(0, near)
    row_copy(0, True).wait_recv()
    row_copy(1, True).wait_recv()
    go(row_copy(2))
    go(row_copy(3))
    arrive(1, near)
    send(1, far)
    forward_to_sibling(1, near)
    arrive(0, far)
    send(4, near)
    forward_to_sibling(0, far)
    row_copy(2, True).wait_recv()
    row_copy(3, True).wait_recv()
    arrive(2, near)
    send(2, far)
    forward_to_sibling(2, near)
    sib_own(1).wait_recv()
    sib_arrive(0, near)
    sib_arrive(1, near)
    units(3, lambda i: (1, 0, i + 3))
    arrive(3, near)
    send(3, far)
    forward_to_sibling(3, near)
    units(4, lambda i: (2 + i // 2, 1 + 2 * (i % 2), 0))
    arrive(1, far)
    forward_to_sibling(1, far)
    sib_arrive(2, near)
    sib_arrive(3, near)
    units(4, lambda i: (2 + i // 4, 1 + 2 * (i % 2), 1 + 2 * ((i // 2) % 2)))
    arrive(4, near)
    send(4, far)
    forward_to_sibling(4, near)
    units(4, lambda i: (3, 1 + 2 * (i % 2), 1 + 2 * ((i // 2) % 2)))
    arrive(2, far)
    forward_to_sibling(2, far)
    arrive(3, far)
    forward_to_sibling(3, far)
    sib_arrive(0, far)
    sib_arrive(1, far)
    units(2, lambda i: (1, 2 * i, 2 * (1 - i)))
    arrive(4, far)
    forward_to_sibling(4, far)
    sib_arrive(2, far)
    sib_arrive(3, far)
    sib_arrive(4, near)
    units(4, lambda i: (2 + i // 2, 1 + 2 * (i % 2), 2))
    sib_arrive(4, far)
    units(3, lambda i: (1, 2, i + 1))

    def reduce_stats(step, carry):
        q, r, g = step // 8, (step // 2) % 4, step % 2
        these = pl.ds(pl.multiple_of(r * count + g * 128, 128), 128)
        m_t = run_max[q, these, :].T
        s_t = run_sum[q, these, :].T
        top = jnp.max(m_t, axis=0, keepdims=True)
        total = jnp.sum(s_t * jnp.exp2(m_t - top), axis=0, keepdims=True)
        lanes = pl.ds(pl.multiple_of(g * 128, 128), 128)
        part[y, r, q, :, lanes] = top
        part[y, r, q + 3, :, lanes] = total
        return carry

    lax.fori_loop(0, 24, reduce_stats, 0)

    def part_copy(shift, owner):
        region = part.at[owner]
        return remote(region, region, part_send.at[shift - 1], part_recv.at[shift - 1], device(dy=shift))

    for shift in (2, 1, 3):
        go(part_copy(shift, y))
    for shift in (1, 3, 2):
        part_copy(shift, (y + 4 - shift) % 4).wait_recv()
    for q in range(3):
        top = part[0, :, q]
        for member in range(1, 4):
            top = jnp.maximum(top, part[member, :, q])
        total = jnp.zeros_like(top)
        for member in range(4):
            total = total + part[member, :, q + 3] * jnp.exp2(part[member, :, q] - top)
        row_lse[q] = top + jnp.log2(total)
        own_lse[q] = row_lse[q, y]

    my_block = x_hi * 4 + z

    def lse_copy(q, block, source):
        to = {"dp": ((block % 4) * 4 + y) * 2 + block // 4, "mod": partner(q)}
        return remote(
            own_lse.at[q - 1], col_lse.at[q - 1, source], lse_send.at[q - 1, block], lse_recv.at[q - 1, source], to
        )

    for q in (1, 2, 3):
        for block in range(8):
            go(lse_copy(q, block, my_block))

    def spread(step, carry):
        q, r, g = step // 8, (step // 2) % 4, step % 2
        lanes = pl.ds(pl.multiple_of(g * 128, 128), 128)
        these = pl.ds(pl.multiple_of(r * count + g * 128, 128), 128)
        value = jnp.broadcast_to(row_lse[q, r, :, lanes], (128, 128))
        run_max[q, these, :] = value.T
        return carry

    lax.fori_loop(0, 24, spread, 0)
    loss = jnp.zeros((1, count), F32)
    eye = lax.broadcasted_iota(jnp.int32, (count, count), 0) == lax.broadcasted_iota(jnp.int32, (count, count), 1)
    own_rows = pl.ds(pl.multiple_of(y * count, count), count)
    own_cols = pl.ds(pl.multiple_of(my_block * count, count), count)
    for q in range(3):
        tile = scores[q, own_rows, own_cols]
        diagonal = jnp.sum(jnp.where(eye, tile, 0.0), axis=0, keepdims=True)
        loss = loss + (own_lse[q] - diagonal) * LN2
    loss_ref[...] = loss

    for q in (1, 2, 3):
        for block in range(8):
            lse_copy(q, block, block).wait_recv()

    span = 4

    def product(r):
        these = pl.ds(pl.multiple_of(r * count, count), count)

        def body(step, carry):
            q, c = step // (8 // span) + 1, step % (8 // span)
            p = partner(q)
            pieces = []
            row_value = run_max[q - 1, these, :]
            for b in range(span):
                column = col_lse[q - 1, c * span + b]
                for lane in range(0, count, 128):
                    t = scores[q - 1, these, pl.ds(pl.multiple_of((c * span + b) * count + lane, 128), 128)]
                    w = jnp.exp2(t - row_value) + jnp.exp2(t - column[:, lane:lane + 128])
                    pieces.append(w.astype(BF16))
            weights = jnp.concatenate(pieces, axis=1)
            here = pl.ds(pl.multiple_of(c * (span * count), span * count), span * count)
            out = factor(q) * jnp.dot(weights, cols[p, here, :], preferred_element_type=F32)
            acc[r] = acc[r] + out
            return carry

        acc[r] = jnp.zeros((count, width), F32)
        lax.fori_loop(0, 3 * (8 // span), body, 0)

    up, down, across = (y + 1) % 4, (y + 3) % 4, (y + 2) % 4

    def rs_copy(kind, src, dst, way):
        slot = 0 if way == 1 else 1
        return remote(src, dst, rs_send.at[slot, kind], rs_recv.at[slot, kind], device(dy=way))

    lower, upper = pl.ds(0, half), pl.ds(half, half)
    product(across)
    stage[0] = acc[across].astype(PART)
    go(rs_copy(0, stage.at[0, lower, :], relay.at[0], 1))
    go(rs_copy(0, stage.at[0, upper, :], relay.at[1], -1))
    product(up)
    stage[1, half:, :] = acc[up, half:, :].astype(PART)
    go(rs_copy(1, stage.at[1, upper, :], final.at[0, upper, :], 1))
    product(down)
    stage[2, :half, :] = acc[down, :half, :].astype(PART)
    go(rs_copy(1, stage.at[2, lower, :], final.at[1, lower, :], -1))
    rs_copy(0, relay.at[0], relay.at[0], 1).wait_recv()
    stage[1, :half, :] = (acc[up, :half, :] + relay[0].astype(F32)).astype(PART)
    go(rs_copy(2, stage.at[1, lower, :], final.at[0, lower, :], 1))
    rs_copy(0, relay.at[1], relay.at[1], -1).wait_recv()
    stage[2, half:, :] = (acc[down, half:, :] + relay[1].astype(F32)).astype(PART)
    go(rs_copy(2, stage.at[2, upper, :], final.at[1, upper, :], -1))
    product(y)
    own = jnp.zeros((count, width), F32)
    for q in (1, 2, 3):
        own = own + (2.0 * factor(q)) * cols[partner(q), own_cols, :].astype(F32)
    acc[y] = acc[y] - own
    rs_copy(1, final.at[0, upper, :], final.at[0, upper, :], 1).wait_recv()
    rs_copy(1, final.at[1, lower, :], final.at[1, lower, :], -1).wait_recv()
    rs_copy(2, final.at[0, lower, :], final.at[0, lower, :], 1).wait_recv()
    rs_copy(2, final.at[1, upper, :], final.at[1, upper, :], -1).wait_recv()
    grad_ref[...] = acc[y] + (final[0].astype(F32) + final[1].astype(F32))
    for copy in started:
        copy.wait_send()


def solution(mesh):
    def shards(embeddings, pairings, logit_scale):
        _, count, width = embeddings.shape
        dma = pltpu.SemaphoreType.DMA
        grad, loss = pl.pallas_call(
            kernel,
            out_shape=(
                jax.ShapeDtypeStruct((count, width), F32),
                jax.ShapeDtypeStruct((1, count), F32),
            ),
            in_specs=[
                pl.BlockSpec(memory_space=pltpu.SMEM),
                pl.BlockSpec(memory_space=pltpu.SMEM),
                pl.BlockSpec(memory_space=pltpu.VMEM),
            ],
            out_specs=(pl.BlockSpec(memory_space=pltpu.VMEM), pl.BlockSpec(memory_space=pltpu.VMEM)),
            scratch_shapes=[
                pltpu.VMEM((4, 8 * count, width), BF16),
                pltpu.VMEM((4, count, width), BF16),
                pltpu.VMEM((3, 4 * count, 8 * count), F32),
                pltpu.VMEM((3, 4 * count, 128), F32),
                pltpu.VMEM((3, 4 * count, 128), F32),
                pltpu.VMEM((4, count, width), F32),
                pltpu.VMEM((3, count, width), PART),
                pltpu.VMEM((2, count // 2, width), PART),
                pltpu.VMEM((2, count, width), PART),
                pltpu.VMEM((4, 4, 6, 1, count), F32),
                pltpu.VMEM((3, 1, count), F32),
                pltpu.VMEM((3, 8, 1, count), F32),
                pltpu.VMEM((3, 4, 1, count), F32),
                dma((2,)),
                dma((2, 5, 4)),
                dma((2, 5, 4)),
                dma((2, 6, 4)),
                dma((2, 6, 4)),
                dma((4,)),
                dma((4,)),
                dma((3,)),
                dma((3,)),
                dma((3, 8)),
                dma((3, 8)),
                dma((2, 3)),
                dma((2, 3)),
            ],
            compiler_params=pltpu.CompilerParams(
                collective_id=0, has_side_effects=True, vmem_limit_bytes=60 * 1024 * 1024
            ),
        )(pairings, logit_scale, embeddings[0])
        return grad[None], loss

    return jax.shard_map(
        shards,
        mesh=mesh,
        in_specs=(P("mod", "dp", None), P(), P()),
        out_specs=(P("mod", "dp", None), P("mod", "dp")),
        check_vma=False,
    )
```

time: 908 us -> 91.5 us (0.10)
  waiting for transfers between devices: 625 us -> 0 us
  blocking collectives: 180 us -> 0 us
  Pallas kernels: 0 us -> 87.8 us
  matrix products: 56.1 us -> 0 us
  other arithmetic: 22.1 us -> 0 us
  between operations: 19.9 us -> 0.65 us
    psum x1 -> x0, waiting for transfers between devices: 312 us -> none  [shards(): col_sum = lax.psum(jnp.sum(jnp.exp(scores - col_max[None, :]), 0), 'dp')]
    all_gather x4 -> x0, waiting for transfers between devices: 311 us -> none  [the longest x3 294 us: shards(): partner = lax.all_gather(own_rows, 'dp', axis=0, tiled=True)]
    pmax x1 -> x0, blocking collectives: 180 us -> none  [shards(): lax.pmax(jnp.max(scores, 0).astype(jnp.bfloat16), 'dp').astype(jnp.float32)]
    pallas_call x0 -> x1, Pallas kernels: none -> 87.8 us  [shards(): pl.pallas_call(kernel, out_shape=(jax.ShapeDtypeStruct((count, width), F3...]
    dot_general x6 -> x0, matrix products: 56.1 us -> none  [the longest x3 28.8 us: shards(): lax.dot_general(anchor, partner, (((1,), (1,)), ((), ())), preferred_elem...]
    reduce_sum x4 -> x0, other arithmetic: 17.4 us -> none  [the longest x3 15.3 us: shards(): row_lse = row_max[:, 0] + jnp.log(jnp.sum(jnp.exp(scores - row_max), 1))]
  transfers between devices with their start and end apart: 5 -> 0, of which waited for: 5 -> 0; matrix products, arithmetic and copies ran while one was open for 3% -> 0% of each run, Pallas kernels for 0% -> 0%
where the time goes in v2:
time: 91.5 us; the launch traced here: 90.8 us
  Pallas kernels  87.8 us (96%)
  local copies, waits for them, and re-layouts  2.44 us (3%)
    pallas_call x1, Pallas kernels, shards(): pl.pallas_call(kernel, out_shape=(jax.ShapeDtypeStruct((count, width), F3...  87.8 us
    unnamed x4, local copies, waits for them, and re-layouts  2.44 us

profile of v2, /device:TPU:0, one launch (start us, length us, event | category | flops | bytes accessed | tf_op | source)
XLA Modules:
  0.0 90.8 jit_solution(2838416954210294064)
XLA Ops:
  0.6 87.8 %shard_map.50 = (f32[256,512]{1,0:T(8,128)}, f32[1,256]{1,0:T(1,128)}) custom-call(s32[3,4]{1,0:T(4,128)} %pair_ref.1, f32[3]{0:T(128)} %scale_ref.1, bf16[256,512]{1,0:T(8,128)(2,1)} %bitcast.3), custom_call_target="tpu_custom_call" | custom-call | tf_op jit(solution)/shard_map/pallas_call | solution.py:370
  88.4 0.0 copy-start
  88.4 1.9 %copy.7 = f32[1,256,512]{2,1,0:T(8,128)} copy(f32[1,256,512]{2,1,0:T(8,128)} %bitcast.2) | data formatting | bytes 1048576
  90.3 0.0 copy-done
  90.3 0.6 copy.8
Async XLA Ops:
  88.4 1.9 %copy-start = (f32[1,256]{1,0:T(1,128)S(1)}, f32[1,256]{1,0:T(1,128)}, u32[]{:S(2)}) copy-start(f32[1,256]{1,0:T(1,128)} %get-tuple-element.9) | copy-start | bytes 3076

commit v3 on v2

v3 whole, which is shorter than its diff:
```python
import functools
import math

import jax
import jax.numpy as jnp
from jax import lax
from jax.experimental import pallas as pl
from jax.experimental.pallas import tpu as pltpu
from jax.sharding import PartitionSpec as P

MESH = pl.DeviceIdType.MESH
F32 = jnp.float32
BF16 = jnp.bfloat16
LN2 = math.log(2.0)
LOG2E = 1.0 / LN2
PART = BF16


def kernel(
    pair_ref, scale_ref, emb_ref, grad_ref, loss_ref,
    cols, rows, scores, run_max, run_sum, acc, stage, relay, final,
    part_a, part_b, own_lse, col_lse, row_lse,
    local_sem, ag_send, ag_recv, sib_send, sib_recv, row_send, row_recv,
    part_send, part_recv, lse_send, lse_recv, rs_send, rs_recv,
):
    count, width = emb_ref.shape
    half, quarter = count // 2, count // 4
    dp = lax.axis_index("dp")
    mod = lax.axis_index("mod")
    x_hi, y, z = dp % 2, (dp // 2) % 4, dp // 8
    core, x_lo = mod % 2, mod // 2
    x = x_hi * 2 + x_lo

    def device(dx=0, dy=0, dz=0, dc=0):
        xx, yy, zz, cc = (x + dx) % 4, (y + dy) % 4, (z + dz) % 4, (core + dc) % 2
        return {"dp": (zz * 4 + yy) * 2 + xx // 2, "mod": (xx % 2) * 2 + cc}

    def partner(q):
        return ((x_lo + q // 2) % 2) * 2 + (core + q % 2) % 2

    def factor(q):
        p = partner(q)
        total = jnp.float32(0.0)
        for k in range(3):
            total = total + jnp.where(pair_ref[k, mod] == p, scale_ref[k], jnp.float32(0.0))
        return total

    def remote(src, dst, send, recv, to):
        return pltpu.make_async_remote_copy(
            src_ref=src, dst_ref=dst, send_sem=send, recv_sem=recv, device_id=to, device_id_type=MESH
        )

    barrier = pltpu.get_barrier_semaphore()
    peers = [device(dx=1), device(dx=3), device(dy=1), device(dy=3), device(dz=1), device(dz=3), device(dc=1)]
    for peer in peers:
        pl.semaphore_signal(barrier, inc=1, device_id=peer, device_id_type=MESH)

    def block_of(dx, dz):
        xx, zz = (x + dx) % 4, (z + dz) % 4
        return xx % 2, (xx // 2) * 4 + zz

    def piece(dx, dz, start, size, dc=0):
        lo, block = block_of(dx, dz)
        return cols.at[lo * 2 + (core + dc) % 2, pl.ds(pl.multiple_of(block * count + start, 64), size), :]

    fill_cols = pltpu.make_async_copy(emb_ref, piece(0, 0, 0, count), local_sem.at[0])
    fill_rows = pltpu.make_async_copy(emb_ref, rows.at[y], local_sem.at[1])
    fill_cols.start()
    fill_rows.start()
    run_max[...] = jnp.full(run_max.shape, -1e30, F32)
    run_sum[...] = jnp.zeros(run_sum.shape, F32)
    acc[...] = jnp.zeros(acc.shape, F32)
    pl.semaphore_wait(barrier, len(peers))

    EVENTS = ((-1, 0, half, 1), (1, 0, half, -1), (2, 0, quarter, 1), (2, quarter, quarter, -1))

    def offsets(h, a, b):
        return (a, b) if h == 0 else (b, a)

    def place(h, group, event):
        rel, start, size, way = EVENTS[event]
        a, b = (rel, 0) if group == 0 else ((0, -1, 1, 2)[group - 1], rel)
        dx, dz = offsets(h, a, b)
        along_x = (group == 0) == (h == 0)
        return dx, dz, h * half + start, size, way, along_x

    def ag_copy(h, group, event):
        dx, dz, start, size, way, along_x = place(h, group, event)
        to = device(dx=way) if along_x else device(dz=way)
        sx, sz = (dx + way, dz) if along_x else (dx, dz + way)
        src = piece(sx, sz, start, size)
        if group in (0, 1) and event in (0, 1):
            src = emb_ref.at[pl.ds(start, size), :]
        return remote(src, piece(sx, sz, start, size), ag_send.at[h, group, event], ag_recv.at[h, group, event], to)

    def ag_arrival(h, group, event):
        dx, dz, start, size, _, _ = place(h, group, event)
        region = piece(dx, dz, start, size)
        return remote(region, region, ag_send.at[h, group, event], ag_recv.at[h, group, event], device(dc=1))

    def sib_copy(h, group, event, dc=0):
        dx, dz, start, size, _, _ = place(h, group, event)
        region = piece(dx, dz, start, size, dc)
        return remote(region, region, sib_send.at[h, group, event], sib_recv.at[h, group, event], device(dc=1))

    def sib_own(dc=0):
        region = piece(0, 0, 0, count, dc)
        src = region if dc else emb_ref
        return remote(src, region, sib_send.at[0, 5, 0], sib_recv.at[0, 5, 0], device(dc=1))

    row_spans = ((1, 0, count, 1), (-1, 0, count, -1), (2, 0, half, 1), (2, half, half, -1))

    def row_copy(event, arrival=False):
        rel, start, size, way = row_spans[event]
        owner = y - way if event >= 2 else y
        if arrival:
            owner = y + (2 if event >= 2 else -way)
        region = rows.at[(owner + 4) % 4, pl.ds(start, size), :]
        src = emb_ref if event < 2 and not arrival else region
        return remote(src, region, row_send.at[event], row_recv.at[event], device(dy=way))

    started = []

    def go(copy):
        copy.start()
        started.append(copy)

    def to_sibling(*triples):
        for triple in triples:
            go(sib_copy(*triple))

    def arrive(*triples):
        for triple in triples:
            ag_arrival(*triple).wait_recv()

    def send(*triples):
        for triple in triples:
            go(ag_copy(*triple))

    def sib_arrive(*triples):
        for triple in triples:
            sib_copy(*triple, 1).wait_recv()

    def near(h, group):
        return (h, group, 0), (h, group, 1)

    def far(h, group):
        return (h, group, 2), (h, group, 3)

    def pairs(n, decode):
        def body(i, carry):
            q, dx0, dz0, dx1, dz1 = decode(i)
            p = partner(q)
            scale = factor(q) * jnp.float32(LOG2E)
            heres = []
            for dx, dz in ((dx0, dz0), (dx1, dz1)):
                heres.append(pl.ds(pl.multiple_of(block_of(dx, dz)[1] * count, count), count))
            for r in range(4):
                these = pl.ds(r * count, count)
                lanes = []
                for here in heres:
                    t = scale * lax.dot_general(
                        rows[r], cols[p, here, :], (((1,), (1,)), ((), ())), preferred_element_type=F32
                    )
                    scores[q - 1, these, here] = t
                    lanes += [t[:, lane:lane + 128] for lane in range(0, count, 128)]
                old = run_max[q - 1, these, :]
                new = old
                for t in lanes:
                    new = jnp.maximum(new, t)
                total = run_sum[q - 1, these, :] * jnp.exp2(old - new)
                for t in lanes:
                    total = total + jnp.exp2(t - new)
                run_max[q - 1, these, :] = new
                run_sum[q - 1, these, :] = total
            return carry

        lax.fori_loop(0, n, body, 0)

    def reduce_stats(first, n, part):
        def body(step, carry):
            q, r = step // 4, step % 4
            for g in range(count // 128):
                these = pl.ds(pl.multiple_of(r * count + g * 128, 128), 128)
                m_t = run_max[first - 1 + q, these, :].T
                s_t = run_sum[first - 1 + q, these, :].T
                top = jnp.max(m_t, axis=0, keepdims=True)
                total = jnp.sum(s_t * jnp.exp2(m_t - top), axis=0, keepdims=True)
                lanes = pl.ds(g * 128, 128)
                part[y, r, q, :, lanes] = top
                part[y, r, q + n, :, lanes] = total
            return carry

        lax.fori_loop(0, n * 4, body, 0)

    def part_copy(part, sem, shift, owner):
        region = part.at[owner]
        return remote(region, region, part_send.at[sem, shift - 1], part_recv.at[sem, shift - 1], device(dy=shift))

    def send_part(part, sem):
        for shift in (2, 1, 3):
            go(part_copy(part, sem, shift, y))

    my_block = x_hi * 4 + z

    def lse_copy(q, block, source):
        to = {"dp": ((block % 4) * 4 + y) * 2 + block // 4, "mod": partner(q)}
        return remote(
            own_lse.at[q - 1], col_lse.at[q - 1, source], lse_send.at[q - 1, block], lse_recv.at[q - 1, source], to
        )

    def combine(first, n, part, sem):
        for shift in (1, 3, 2):
            part_copy(part, sem, shift, (y + 4 - shift) % 4).wait_recv()
        for q in range(n):
            top = part[0, :, q]
            for member in range(1, 4):
                top = jnp.maximum(top, part[member, :, q])
            total = jnp.zeros_like(top)
            for member in range(4):
                total = total + part[member, :, q + n] * jnp.exp2(part[member, :, q] - top)
            row_lse[first - 1 + q] = top + jnp.log2(total)
            own_lse[first - 1 + q] = row_lse[first - 1 + q, y]
        for q in range(first, first + n):
            for block in range(8):
                go(lse_copy(q, block, my_block))

        def spread(step, carry):
            q, r = first - 1 + step // 4, step % 4
            for g in range(count // 128):
                lanes = pl.ds(g * 128, 128)
                these = pl.ds(pl.multiple_of(r * count + g * 128, 128), 128)
                value = jnp.broadcast_to(row_lse[q, r, :, lanes], (128, 128))
                run_max[q, these, :] = value.T
            return carry

        lax.fori_loop(0, 4 * n, spread, 0)

    def columns_arrive(first, n):
        for q in range(first, first + n):
            for block in range(8):
                lse_copy(q, block, block).wait_recv()

    def product(q, r):
        these = pl.ds(pl.multiple_of(r * count, count), count)
        row_value = run_max[q - 1, these, :]
        pieces = []
        for block in range(8):
            column = col_lse[q - 1, block]
            for lane in range(0, count, 128):
                t = scores[q - 1, these, block * count + lane:block * count + lane + 128]
                w = jnp.exp2(t - row_value) + jnp.exp2(t - column[:, lane:lane + 128])
                pieces.append(w.astype(BF16))
        out = jnp.dot(jnp.concatenate(pieces, axis=1), cols[partner(q)], preferred_element_type=F32)
        acc[r] = acc[r] + factor(q) * out

    send(*near(0, 0), *near(1, 0))
    go(sib_own())
    go(row_copy(0))
    go(row_copy(1))
    send(*near(1, 1), *near(0, 1))
    fill_cols.wait()
    fill_rows.wait()
    arrive(*near(0, 0), *near(1, 0))
    send(*far(1, 0), *near(1, 2), *near(0, 2), *far(0, 0), *near(0, 3), *near(1, 3))
    to_sibling(*near(0, 0), *near(1, 0))
    arrive(*near(0, 1), *near(1, 1))
    to_sibling(*near(1, 1), *near(0, 1))
    row_copy(0, True).wait_recv()
    row_copy(1, True).wait_recv()
    go(row_copy(2))
    go(row_copy(3))
    arrive(*far(1, 0))
    send(*near(1, 4))
    to_sibling(*far(1, 0))
    arrive(*near(1, 2))
    to_sibling(*near(1, 2))
    arrive(*near(0, 2))
    send(*far(0, 2))
    to_sibling(*near(0, 2))
    arrive(*far(0, 0))
    to_sibling(*far(0, 0))
    row_copy(2, True).wait_recv()
    row_copy(3, True).wait_recv()
    sib_arrive(*near(0, 0), *near(1, 1))
    pairs(2, lambda i: (2 + i, 1, 0, 3, 0))
    arrive(*near(0, 3))
    send(*far(0, 3), *near(0, 4), *far(0, 1))
    to_sibling(*near(0, 3))
    arrive(*near(1, 3))
    send(*far(1, 1), *far(1, 2), *far(1, 3))
    to_sibling(*near(1, 3))
    pairs(2, lambda i: (2, 1, 1 + 2 * i, 3, 1 + 2 * i))
    sib_arrive(*near(0, 2), *near(0, 3), *near(1, 2), *near(1, 3))
    pairs(1, lambda i: (3, 1, 1, 3, 1))
    arrive(*near(1, 4))
    send(*far(1, 4))
    to_sibling(*near(1, 4))
    arrive(*far(0, 2), *far(0, 3))
    to_sibling(*far(0, 2), *far(0, 3))
    pairs(2, lambda i: (3 - i, 1, 3 - i, 3, 3 - i))
    sib_arrive(*near(1, 4), *far(0, 2), *far(0, 3))
    pairs(1, lambda i: (3, 1, 2, 3, 2))
    arrive(*near(0, 4))
    send(*far(0, 4))
    to_sibling(*near(0, 4))
    reduce_stats(2, 2, part_a)
    send_part(part_a, 0)
    arrive(*far(1, 1), *far(0, 1), *far(1, 2))
    to_sibling(*far(1, 1), *far(0, 1), *far(1, 2))
    sib_own(1).wait_recv()
    sib_arrive(*near(1, 0), *near(0, 1))
    pairs(1, lambda i: (1, 0, 1, 0, 3))
    arrive(*far(1, 3))
    to_sibling(*far(1, 3))
    sib_arrive(*far(1, 0), *far(0, 0), *far(1, 1), *far(0, 1))
    pairs(1, lambda i: (1, 0, 2, 2, 0))
    arrive(*far(1, 4), *far(0, 4))
    to_sibling(*far(1, 4), *far(0, 4))
    sib_arrive(*near(0, 4), *far(1, 2), *far(1, 3))
    pairs(1, lambda i: (1, 2, 1, 2, 3))
    sib_arrive(*far(1, 4), *far(0, 4))
    pairs(1, lambda i: (1, 0, 0, 2, 2))
    reduce_stats(1, 1, part_b)
    send_part(part_b, 1)
    combine(2, 2, part_a, 0)
    combine(1, 1, part_b, 1)

    loss = jnp.zeros((1, count), F32)
    eye = lax.broadcasted_iota(jnp.int32, (count, count), 0) == lax.broadcasted_iota(jnp.int32, (count, count), 1)
    own_rows = pl.ds(pl.multiple_of(y * count, count), count)
    own_cols = pl.ds(pl.multiple_of(my_block * count, count), count)
    for q in range(3):
        tile = scores[q, own_rows, own_cols]
        diagonal = jnp.sum(jnp.where(eye, tile, 0.0), axis=0, keepdims=True)
        loss = loss + (own_lse[q] - diagonal) * LN2
    loss_ref[...] = loss
    own = jnp.zeros((count, width), F32)
    for q in (1, 2, 3):
        own = own + (2.0 * factor(q)) * cols[partner(q), own_cols, :].astype(F32)
    acc[y] = acc[y] - own

    up, down, across = (y + 1) % 4, (y + 3) % 4, (y + 2) % 4

    def rs_copy(kind, src, dst, way):
        slot = 0 if way == 1 else 1
        return remote(src, dst, rs_send.at[slot, kind], rs_recv.at[slot, kind], device(dy=way))

    lower, upper = pl.ds(0, half), pl.ds(half, half)

    def early(step, carry):
        i = step // 2
        product(2 + step % 2, (y + 2 - i + 3 * (i // 2)) % 4)
        return carry

    def late(q, r):
        def body(step, carry):
            product(q + step, r)
            return carry
        return body

    columns_arrive(2, 2)
    lax.fori_loop(0, 6, early, 0)
    columns_arrive(1, 1)
    lax.fori_loop(0, 1, late(1, across), 0)
    stage[0] = acc[across].astype(PART)
    go(rs_copy(0, stage.at[0, lower, :], relay.at[0], 1))
    go(rs_copy(0, stage.at[0, upper, :], relay.at[1], -1))
    lax.fori_loop(0, 1, late(1, up), 0)
    stage[1, half:, :] = acc[up, half:, :].astype(PART)
    go(rs_copy(1, stage.at[1, upper, :], final.at[0, upper, :], 1))
    lax.fori_loop(0, 1, late(1, down), 0)
    stage[2, :half, :] = acc[down, :half, :].astype(PART)
    go(rs_copy(1, stage.at[2, lower, :], final.at[1, lower, :], -1))
    lax.fori_loop(0, 1, late(1, y), 0)
    rs_copy(0, relay.at[0], relay.at[0], 1).wait_recv()
    stage[1, :half, :] = (acc[up, :half, :] + relay[0].astype(F32)).astype(PART)
    go(rs_copy(2, stage.at[1, lower, :], final.at[0, lower, :], 1))
    rs_copy(0, relay.at[1], relay.at[1], -1).wait_recv()
    stage[2, half:, :] = (acc[down, half:, :] + relay[1].astype(F32)).astype(PART)
    go(rs_copy(2, stage.at[2, upper, :], final.at[1, upper, :], -1))
    lax.fori_loop(0, 2, late(2, y), 0)
    rs_copy(1, final.at[0, upper, :], final.at[0, upper, :], 1).wait_recv()
    rs_copy(1, final.at[1, lower, :], final.at[1, lower, :], -1).wait_recv()
    rs_copy(2, final.at[0, lower, :], final.at[0, lower, :], 1).wait_recv()
    rs_copy(2, final.at[1, upper, :], final.at[1, upper, :], -1).wait_recv()
    grad_ref[...] = acc[y] + (final[0].astype(F32) + final[1].astype(F32))
    for copy in started:
        copy.wait_send()


def solution(mesh):
    def shards(embeddings, pairings, logit_scale):
        _, count, width = embeddings.shape
        dma = pltpu.SemaphoreType.DMA
        grad, loss = pl.pallas_call(
            kernel,
            out_shape=(
                jax.ShapeDtypeStruct((count, width), F32),
                jax.ShapeDtypeStruct((1, count), F32),
            ),
            in_specs=[
                pl.BlockSpec(memory_space=pltpu.SMEM),
                pl.BlockSpec(memory_space=pltpu.SMEM),
                pl.BlockSpec(memory_space=pltpu.VMEM),
            ],
            out_specs=(pl.BlockSpec(memory_space=pltpu.VMEM), pl.BlockSpec(memory_space=pltpu.VMEM)),
            scratch_shapes=[
                pltpu.VMEM((4, 8 * count, width), BF16),
                pltpu.VMEM((4, count, width), BF16),
                pltpu.VMEM((3, 4 * count, 8 * count), F32),
                pltpu.VMEM((3, 4 * count, 128), F32),
                pltpu.VMEM((3, 4 * count, 128), F32),
                pltpu.VMEM((4, count, width), F32),
                pltpu.VMEM((3, count, width), PART),
                pltpu.VMEM((2, count // 2, width), PART),
                pltpu.VMEM((2, count, width), PART),
                pltpu.VMEM((4, 4, 4, 1, count), F32),
                pltpu.VMEM((4, 4, 2, 1, count), F32),
                pltpu.VMEM((3, 1, count), F32),
                pltpu.VMEM((3, 8, 1, count), F32),
                pltpu.VMEM((3, 4, 1, count), F32),
                dma((2,)),
                dma((2, 5, 4)),
                dma((2, 5, 4)),
                dma((2, 6, 4)),
                dma((2, 6, 4)),
                dma((4,)),
                dma((4,)),
                dma((2, 3)),
                dma((2, 3)),
                dma((3, 8)),
                dma((3, 8)),
                dma((2, 3)),
                dma((2, 3)),
            ],
            compiler_params=pltpu.CompilerParams(
                collective_id=0, has_side_effects=True, vmem_limit_bytes=60 * 1024 * 1024
            ),
        )(pairings, logit_scale, embeddings[0])
        return grad[None], loss

    return jax.shard_map(
        shards,
        mesh=mesh,
        in_specs=(P("mod", "dp", None), P(), P()),
        out_specs=(P("mod", "dp", None), P("mod", "dp")),
        check_vma=False,
    )
```

time: 91.5 us -> 64.4 us (0.70)
  Pallas kernels: 87.8 us -> 60.6 us
    pallas_call x1, Pallas kernels: 87.8 us -> 60.6 us  [shards(): pl.pallas_call(kernel, out_shape=(jax.ShapeDtypeStruct((count, width), F3...]
where the time goes in v3:
time: 64.4 us; the launch traced here: 63.7 us
  Pallas kernels  60.6 us (94%)
  local copies, waits for them, and re-layouts  2.44 us (4%)
  between operations  0.65 us (1%)
    pallas_call x1, Pallas kernels, shards(): pl.pallas_call(kernel, out_shape=(jax.ShapeDtypeStruct((count, width), F3...  60.6 us
    unnamed x4, local copies, waits for them, and re-layouts  2.44 us

profile of v3, /device:TPU:0, one launch (start us, length us, event | category | flops | bytes accessed | tf_op | source)
XLA Modules:
  0.0 63.7 jit_solution(17592459719720989833)
XLA Ops:
  0.6 60.6 %shard_map.50 = (f32[256,512]{1,0:T(8,128)}, f32[1,256]{1,0:T(1,128)}) custom-call(s32[3,4]{1,0:T(4,128)} %pair_ref.1, f32[3]{0:T(128)} %scale_ref.1, bf16[256,512]{1,0:T(8,128)(2,1)} %bitcast.3), custom_call_target="tpu_custom_call" | custom-call | tf_op jit(solution)/shard_map/pallas_call | solution.py:396
  61.3 0.0 copy-start
  61.3 1.9 %copy.7 = f32[1,256,512]{2,1,0:T(8,128)} copy(f32[1,256,512]{2,1,0:T(8,128)} %bitcast.2) | data formatting | bytes 1048576
  63.2 0.0 copy-done
  63.2 0.6 copy.8
Async XLA Ops:
  61.3 1.9 %copy-start = (f32[1,256]{1,0:T(1,128)S(1)}, f32[1,256]{1,0:T(1,128)}, u32[]{:S(2)}) copy-start(f32[1,256]{1,0:T(1,128)} %get-tuple-element.9) | copy-start | bytes 3076
